TPU v7x, 512 devices: a whole 4x8x8 slice. The times are simulated.
512 devices in a mesh: fsdp: 64 (over x, z, y_hi), dp: 8 (over y_lo, core).
Axes of the slice: x: 4, y: 8 (y_hi: 2, y_lo: 4; y = y_hi * 4 + y_lo), z: 8, core: 2. Of those that a mesh axis runs over, the one named last changes fastest.
Arguments:
- tokens: bfloat16 [65536, 8192], P(('fsdp', 'dp')), may hold values from -6 to 6
- token_adapter_index: int32 [65536, 1], P(('fsdp', 'dp')), may hold values from 0 to 63; in each aligned block of 128 rows (0 to 127, 128 to 255, ...) at most 3 rows name the same one
- adapter_storage_index: int32 [64], replicated, may hold values from 0 to 63, each once
- frozen_value_weight: bfloat16 [8192, 512], P(('fsdp', 'dp')), may hold values from -0.0625 to 0.0625
- frozen_value_bias: bfloat16 [512], replicated, may hold values from -3 to 3
- adapter_down_weight: bfloat16 [64, 8192, 64], P('fsdp'), may hold values from -0.0625 to 0.0625
- adapter_up_weight: bfloat16 [64, 64, 512], P('fsdp'), may hold values from -0.75 to 0.75
- cotangent: bfloat16 [65536, 512], P(('fsdp', 'dp')), may hold values from -0.1875 to 0.1875
Outputs:
- values: bfloat16 [65536, 512], P(('fsdp', 'dp'))
- grad_down: float32 [64, 8192, 64], P('fsdp', 'dp')
- grad_up: float32 [64, 64, 512], P('fsdp', None, 'dp')
Inputs may be any that keep to these rules, and one draw needn't show every extreme that they name: `token_adapter_index`: within the 128 rows of one device no adapter is named by more than 3 rows. `adapter_storage_index`: each storage index appears once.
All inputs are finite; a program needn't handle non-finite values.
Results may differ from a plain program's by a relative error of at most 0.0048.
Values may be sent and summed in bfloat16 or wider, within the bound.
No kernel may reach another device: no remote copies, remote signals or barrier semaphores. Data moves between devices by JAX's collectives and lax.ppermute only.
A program may use at most 64 MiB of HBM per device.

v0:
```python
import jax
import jax.numpy as jnp
from jax import lax
from jax.sharding import PartitionSpec as P


def body(
    tokens,
    token_adapter_index,
    adapter_storage_index,
    frozen_value_weight,
    frozen_value_bias,
    adapter_down_weight,
    adapter_up_weight,
    cotangent,
):
    token_count, model_width = tokens.shape
    value_width = frozen_value_weight.shape[1]
    fsdp_size = lax.axis_size("fsdp")
    slots_total = adapter_storage_index.shape[0]
    capacity = max(2, (3 * token_count + 2 * fsdp_size - 1) // (2 * fsdp_size))
    base_value = jnp.dot(
        tokens,
        lax.all_gather(frozen_value_weight, ("fsdp", "dp"), axis=0, tiled=True),
        preferred_element_type=jnp.float32,
    )
    base_value = base_value + frozen_value_bias.astype(jnp.float32)
    owner_index = jnp.take(adapter_storage_index, token_adapter_index[:, 0])
    onehot = (owner_index[:, None] == jnp.arange(slots_total)[None, :]).astype(jnp.int32)
    place_in_slot = jnp.sum((jnp.cumsum(onehot, 0) - onehot) * onehot, 1)
    target_row = owner_index * capacity + place_in_slot
    dispatch = (jnp.arange(slots_total * capacity)[:, None] == target_row[None, :]).astype(
        jnp.bfloat16
    )
    sent_rows = jnp.dot(dispatch, tokens, preferred_element_type=jnp.float32).astype(jnp.bfloat16)
    sent_rows = sent_rows.reshape(slots_total, capacity, model_width)
    sent_cot = jnp.dot(dispatch, cotangent, preferred_element_type=jnp.float32).astype(jnp.bfloat16)
    sent_cot = sent_cot.reshape(slots_total, capacity, value_width)
    arrived = lax.all_to_all(sent_rows, "fsdp", split_axis=0, concat_axis=0, tiled=True)
    arrived_rows = arrived.reshape(-1, model_width)
    down_projection = adapter_down_weight[0]
    up_projection = adapter_up_weight[0]
    rank_activation = jnp.dot(
        arrived_rows, down_projection, preferred_element_type=jnp.float32
    ).astype(jnp.bfloat16)
    adapter_delta = jnp.dot(
        rank_activation, up_projection, preferred_element_type=jnp.float32
    ).astype(jnp.bfloat16)
    returned = lax.all_to_all(
        adapter_delta.reshape(fsdp_size, capacity, value_width),
        "fsdp",
        split_axis=0,
        concat_axis=0,
        tiled=True,
    )
    returned = returned.reshape(-1, value_width)
    placed = jnp.einsum("st,sk->tk", dispatch, returned, preferred_element_type=jnp.float32)
    values = (base_value + placed).astype(jnp.bfloat16)
    arrived_cot = lax.all_to_all(sent_cot, "fsdp", split_axis=0, concat_axis=0, tiled=True)
    cotangent_rows = arrived_cot.reshape(-1, value_width)
    rank_cotangent = lax.dot_general(
        cotangent_rows, up_projection, (((1,), (1,)), ((), ())), preferred_element_type=jnp.float32
    ).astype(jnp.bfloat16)
    grad_down = lax.dot_general(
        arrived_rows, rank_cotangent, (((0,), (0,)), ((), ())), preferred_element_type=jnp.float32
    )
    grad_up = lax.dot_general(
        rank_activation,
        cotangent_rows,
        (((0,), (0,)), ((), ())),
        preferred_element_type=jnp.float32,
    )
    summed_down, summed_up = (
        lax.psum_scatter(grad_down, "dp", scatter_dimension=0, tiled=True),
        lax.psum_scatter(grad_up, "dp", scatter_dimension=1, tiled=True),
    )
    return (values, summed_down[None], summed_up[None])


def solution(mesh):
    return jax.shard_map(
        body,
        mesh=mesh,
        in_specs=(
            P(("fsdp", "dp"), None),
            P(("fsdp", "dp"), None),
            P(),
            P(("fsdp", "dp"), None),
            P(),
            P("fsdp", None, None),
            P("fsdp", None, None),
            P(("fsdp", "dp"), None),
        ),
        out_specs=(P(("fsdp", "dp"), None), P("fsdp", "dp", None), P("fsdp", None, "dp")),
        check_vma=False,
    )
```

profile of v0, /device:TPU:1, one launch (start us, length us, event | category | flops | bytes accessed | tf_op | source)
XLA Modules:
  0.0 325.9 jit_solution(2407330163752891406)
XLA Ops:
  8.0 0.0 copy-start
  8.0 0.8 fusion.13
  8.8 1.6 gather_fusion
  10.4 0.7 fusion.12
  11.1 0.1 fusion.6
  11.2 0.2 reduce_window_sum.11
  11.3 0.2 select_reduce_fusion
  11.5 0.7 fusion.11
  12.2 1.1 convolution_convert_fusion.2
  13.3 0.8 reshape.45
  14.1 19.6 %all-to-all-start.2 = ((bf16[64,3,512]{2,1,0:T(4,128)(2,1)}), bf16[64,3,512]{2,1,0:T(4,128)(2,1)S(1)}, u32[]{:S(2)}, u32[]{:S(2)}) async-start(bf16[64,3,512]{2,1,0:T(4,128)(2,1)} %reshape.45), calls=%async_computation.2 | async-start | bytes 524288 | tf_op jit(solution)/shard_map/all_to_all | solution.py:59
  33.7 0.0 copy-done
  33.7 2.6 convolution_convert_fusion
  36.3 7.1 %reshape.41 = bf16[64,3,8192]{2,1,0:T(4,128)(2,1)} reshape(bf16[192,8192]{1,0:T(8,128)(2,1)} %convolution_convert_fusion) | data formatting | bytes 6291456 | tf_op jit(solution)/shard_map/reshape | solution.py:36
  43.4 4.0 %all-to-all-done.2 = bf16[64,3,512]{2,1,0:T(4,128)(2,1)S(1)} async-done(((bf16[64,3,512]{2,1,0:T(4,128)(2,1)}), bf16[64,3,512]{2,1,0:T(4,128)(2,1)S(1)}, u32[]{:S(2)}, u32[]{:S(2)}) %all-to-all-start.2) | async-done | bytes 196640 | tf_op jit(solution)/shard_map/all_to_all | solution.py:59
  47.4 10.9 %all-to-all-start = ((bf16[64,3,8192]{2,1,0:T(4,128)(2,1)}), bf16[64,3,8192]{2,1,0:T(4,128)(2,1)}, u32[]{:S(2)}, u32[]{:S(2)}) async-start(bf16[64,3,8192]{2,1,0:T(4,128)(2,1)} %reshape.41), calls=%async_computation | async-start | bytes 8388608 | tf_op jit(solution)/shard_map/all_to_all | solution.py:39
  58.2 0.0 reduce-scatter.7.cloned.1.call-start
  58.3 0.2 reshape.46
  58.5 0.0 copy-start.1
  58.5 94.7 %all-to-all-done = bf16[64,3,8192]{2,1,0:T(4,128)(2,1)} async-done(((bf16[64,3,8192]{2,1,0:T(4,128)(2,1)}), bf16[64,3,8192]{2,1,0:T(4,128)(2,1)}, u32[]{:S(2)}, u32[]{:S(2)}) %all-to-all-start) | async-done | bytes 3145760 | tf_op jit(solution)/shard_map/all_to_all | solution.py:39
  153.1 7.5 %reshape.42 = bf16[192,8192]{1,0:T(8,128)(2,1)} reshape(bf16[64,3,8192]{2,1,0:T(4,128)(2,1)} %all-to-all-done) | data formatting | bytes 6291456 | tf_op jit(solution)/shard_map/reshape | solution.py:40
  160.6 0.0 copy-done.1
  160.6 0.0 copy-start.2
  160.6 3.0 convolution_convert_fusion.4
  163.6 1.0 convolution_bitcast_fusion
  164.6 0.0 reduce-scatter.7.cloned.1.call-update
  164.6 0.0 all-gather.2.cloned.1.call-start
  164.7 0.5 all-gather.2.cloned.1.call-update
  165.2 0.0 copy-start.3
  165.2 0.0 reduce-scatter.5.cloned.1.call-start
  165.3 0.0 copy-done.2
  165.3 4.2 %fusion.1 = f32[8192,64]{0,1:T(8,128)} fusion(bf16[192,8192]{1,0:T(8,128)(2,1)} %reshape.42, bf16[192,512]{1,0:T(8,128)(2,1)S(1)} %reshape.46, bf16[1,64,512]{2,1,0:T(8,128)(2,1)S(1)} %copy-done.2), kind=kOutput, calls=%fused_computation.10 | convolution fusion | flops 213921792 | bytes 5505024 | tf_op jit(solution)/shard_map/dot_general | solution.py:64
  169.5 0.0 reduce-scatter.5.cloned.1.call-update
  169.6 0.2 convolution_convert_fusion.1
  169.8 0.8 reshape.43
  170.7 13.7 %all-to-all-start.1 = ((bf16[64,3,512]{2,1,0:T(4,128)(2,1)}), bf16[64,3,512]{2,1,0:T(4,128)(2,1)S(1)}, u32[]{:S(2)}, u32[]{:S(2)}) async-start(bf16[64,3,512]{2,1,0:T(4,128)(2,1)} %reshape.43), calls=%async_computation.1 | async-start | bytes 524288 | tf_op jit(solution)/shard_map/all_to_all | solution.py:49
  184.4 0.0 copy-done.3
  184.4 31.2 %reduce-scatter.7.cloned.1.call-done = f32[64,64]{1,0:T(8,128)} async-done(((f32[512,64]{1,0:T(8,128)}), f32[64,64]{1,0:T(8,128)}) %reduce-scatter.7.cloned.1.call-update) | async-done | bytes 16400
  215.6 1.5 copy.12
  217.1 0.0 all-to-all-done.1
  217.1 0.2 reshape.44
  217.2 95.7 %all-gather.2.cloned.1.call-done = bf16[8192,512]{1,0:T(8,128)(2,1)} async-done(((bf16[16,512]{1,0:T(8,128)(2,1)}), bf16[8192,512]{1,0:T(8,128)(2,1)}) %all-gather.2.cloned.1.call-update) | async-done | bytes 8388624 | tf_op jit(solution)/shard_map/all_gather | solution.py:24
  312.9 4.6 %convolution_add_fusion.1 = f32[128,512]{1,0:T(8,128)S(1)} fusion(bf16[128,8192]{1,0:T(8,128)(2,1)S(1)} %copy-done, bf16[8192,512]{1,0:T(8,128)(2,1)} %all-gather.2.cloned.1.call-done, f32[512]{0:T(512)S(1)} %convert_element_type.25), kind=kOutput, calls=%fused_computation.6 | convolution fusion | flops 1073807360 | bytes 10749952 | tf_op jit(solution)/shard_map/dot_general | solution.py:22
  317.6 0.9 fusion
  318.4 0.0 reduce-scatter.5.cloned.1.call-done
  (2 shorter events, 0.0 us)
Async XLA Ops:
  8.0 25.7 %copy-start = (bf16[128,8192]{1,0:T(8,128)(2,1)S(1)}, bf16[128,8192]{1,0:T(8,128)(2,1)}, u32[]{:S(2)}) copy-start(bf16[128,8192]{1,0:T(8,128)(2,1)} %param.8) | copy-start | bytes 6291460
  14.1 33.3 %all-to-all-start.2 = ((bf16[64,3,512]{2,1,0:T(4,128)(2,1)}), bf16[64,3,512]{2,1,0:T(4,128)(2,1)S(1)}, u32[]{:S(2)}, u32[]{:S(2)}) async-start(bf16[64,3,512]{2,1,0:T(4,128)(2,1)} %reshape.45), calls=%async_computation.2 | async-start | bytes 524288 | tf_op jit(solution)/shard_map/all_to_all | solution.py:59
  47.4 105.8 %all-to-all-start = ((bf16[64,3,8192]{2,1,0:T(4,128)(2,1)}), bf16[64,3,8192]{2,1,0:T(4,128)(2,1)}, u32[]{:S(2)}, u32[]{:S(2)}) async-start(bf16[64,3,8192]{2,1,0:T(4,128)(2,1)} %reshape.41), calls=%async_computation | async-start | bytes 8388608 | tf_op jit(solution)/shard_map/all_to_all | solution.py:39
  58.2 157.4 %reduce-scatter.7.cloned.1.call-start = ((), (), s32[]{:S(2)}) async-start(), calls=%async_computation.7 | async-start | bytes 294912
  58.5 102.1 %copy-start.1 = (bf16[1,8192,64]{1,2,0:T(8,128)(2,1)S(1)}, bf16[1,8192,64]{1,2,0:T(8,128)(2,1)}, u32[]{:S(2)}) copy-start(bf16[1,8192,64]{1,2,0:T(8,128)(2,1)} %param.13) | copy-start | bytes 3145732
  160.6 4.7 %copy-start.2 = (bf16[1,64,512]{2,1,0:T(8,128)(2,1)S(1)}, bf16[1,64,512]{2,1,0:T(8,128)(2,1)}, u32[]{:S(2)}) copy-start(bf16[1,64,512]{2,1,0:T(8,128)(2,1)} %param.14) | copy-start | bytes 196612
  164.6 148.3 %all-gather.2.cloned.1.call-start = ((), (), s32[]{:S(2)}) async-start(), calls=%async_computation.5 | async-start | bytes 8404992 | tf_op jit(solution)/shard_map/all_gather | solution.py:24
  165.2 19.1 %copy-start.3 = (bf16[512]{0:T(512)(128)(2,1)S(1)}, bf16[512]{0:T(512)(128)(2,1)}, u32[]{:S(2)}) copy-start(bf16[512]{0:T(512)(128)(2,1)} %param.12) | copy-start | bytes 3076
  165.2 153.2 %reduce-scatter.5.cloned.1.call-start = ((), (), s32[]{:S(2)}) async-start(), calls=%async_computation.6 | async-start | bytes 2359296 | tf_op jit(solution)/shard_map/reduce_scatter | solution.py:74
  170.7 46.4 %all-to-all-start.1 = ((bf16[64,3,512]{2,1,0:T(4,128)(2,1)}), bf16[64,3,512]{2,1,0:T(4,128)(2,1)S(1)}, u32[]{:S(2)}, u32[]{:S(2)}) async-start(bf16[64,3,512]{2,1,0:T(4,128)(2,1)} %reshape.43), calls=%async_computation.1 | async-start | bytes 524288 | tf_op jit(solution)/shard_map/all_to_all | solution.py:49
Sparse Core Ops, SparseCore 0:
  164.8 50.7 reduce-scatter.6
  219.0 43.4 reduce-scatter.4
Sparse Core Ops, SparseCore 1:
  169.6 143.3 all-gather.1
where the time goes:
time: 327 us; the launch traced here: 326 us
  waiting for transfers between devices  226 us (69%)
  starting transfers between devices  44.3 us (14%)
  local copies, waits for them, and re-layouts  19.6 us (6%)
  matrix products  17.7 us (5%)
  between operations  15.6 us (5%)
    all_gather x1, waiting for transfers between devices, body(): lax.all_gather(frozen_value_weight, ('fsdp', 'dp'), axis=0, tiled=True)  95.7 us
    all_to_all x1, waiting for transfers between devices, body(): lax.all_to_all(sent_rows, 'fsdp', split_axis=0, concat_axis=0, tiled=True)  94.7 us
    unnamed x4, waiting for transfers between devices  31.8 us
    all_to_all x1, starting transfers between devices, body(): lax.all_to_all(sent_cot, 'fsdp', split_axis=0, concat_axis=0, tiled=True)  19.6 us
    all_to_all x1, starting transfers between devices, body(): lax.all_to_all(adapter_delta.reshape(fsdp_size, capacity, value_width), '...  13.7 us
    all_to_all x1, starting transfers between devices, body(): lax.all_to_all(sent_rows, 'fsdp', split_axis=0, concat_axis=0, tiled=True)  10.9 us
    reshape x1, local copies, waits for them, and re-layouts, body(): arrived_rows = arrived.reshape(-1, model_width)  7.46 us
    reshape x1, local copies, waits for them, and re-layouts, body(): sent_rows = sent_rows.reshape(slots_total, capacity, model_width)  7.05 us
  transfers between devices with their start and end apart: 6, of which 4 were waited for; matrix products, arithmetic and copies ran while one was open for 7% of the time, Pallas kernels for 0%

commit v1 on v0

--- a/solution.py
+++ b/solution.py
@@ -21,7 +21,15 @@
     capacity = max(2, (3 * token_count + 2 * fsdp_size - 1) // (2 * fsdp_size))
     base_value = jnp.dot(
         tokens,
-        lax.all_gather(frozen_value_weight, ("fsdp", "dp"), axis=0, tiled=True),
+        jnp.concatenate(
+            lax.all_to_all(
+                jnp.stack([frozen_value_weight] * lax.axis_size(("fsdp", "dp"))),
+                ("fsdp", "dp"),
+                0,
+                0,
+            ),
+            axis=0,
+        ),
         preferred_element_type=jnp.float32,
     )
     base_value = base_value + frozen_value_bias.astype(jnp.float32)

time: 327 us -> 436 us (1.33)
  waiting for transfers between devices: 226 us -> 300 us
  blocking collectives: 0 us -> 25.4 us
  starting transfers between devices: 44.3 us -> 53.6 us
    all_to_all x1, waiting for transfers between devices: 0.01 us -> 160 us  [body(): lax.all_to_all(jnp.stack([frozen_value_weight] * lax.axis_size(('fsdp', '...]
    all_gather x1 -> x0, waiting for transfers between devices: 95.7 us -> none  [body(): lax.all_gather(frozen_value_weight, ('fsdp', 'dp'), axis=0, tiled=True)]
    all_to_all x0 -> x1, blocking collectives: none -> 25.4 us  [body(): lax.all_to_all(adapter_delta.reshape(fsdp_size, capacity, value_width), '...]
    all_to_all x1, starting transfers between devices: 13.7 us -> 23.4 us  [body(): lax.all_to_all(jnp.stack([frozen_value_weight] * lax.axis_size(('fsdp', '...]
    all_to_all x1, starting transfers between devices: 19.6 us -> 10.1 us  [body(): lax.all_to_all(sent_cot, 'fsdp', split_axis=0, concat_axis=0, tiled=True)]
    all_to_all x1, starting transfers between devices: 10.9 us -> 20 us  [body(): lax.all_to_all(sent_rows, 'fsdp', split_axis=0, concat_axis=0, tiled=True)]
    unnamed x4 -> x3, waiting for transfers between devices: 31.8 us -> 40.7 us
  transfers between devices with their start and end apart: 6 -> 5, of which waited for: 4 -> 4; matrix products, arithmetic and copies ran while one was open for 7% -> 6% of each run, Pallas kernels for 0% -> 0%
where the time goes in v1:
time: 436 us
  waiting for transfers between devices  300 us (69%)
  starting transfers between devices  53.6 us (12%)
  blocking collectives  25.4 us (6%)
  local copies, waits for them, and re-layouts  23.2 us (5%)
  matrix products  16.8 us (4%)
  between operations  14.2 us (3%)
    all_to_all x1, waiting for transfers between devices, body(): lax.all_to_all(jnp.stack([frozen_value_weight] * lax.axis_size(('fsdp', '...  160 us
    all_to_all x1, waiting for transfers between devices, body(): lax.all_to_all(sent_rows, 'fsdp', split_axis=0, concat_axis=0, tiled=True)  96.4 us
    unnamed x3, waiting for transfers between devices  40.7 us
    all_to_all x1, blocking collectives, body(): lax.all_to_all(adapter_delta.reshape(fsdp_size, capacity, value_width), '...  25.4 us
    all_to_all x1, starting transfers between devices, body(): lax.all_to_all(jnp.stack([frozen_value_weight] * lax.axis_size(('fsdp', '...  23.4 us
    all_to_all x1, starting transfers between devices, body(): lax.all_to_all(sent_rows, 'fsdp', split_axis=0, concat_axis=0, tiled=True)  20 us
    all_to_all x1, starting transfers between devices, body(): lax.all_to_all(sent_cot, 'fsdp', split_axis=0, concat_axis=0, tiled=True)  10.1 us
  transfers between devices with their start and end apart: 5, of which 4 were waited for; matrix products, arithmetic and copies ran while one was open for 6% of the time, Pallas kernels for 0%

profile of v1, /device:TPU:1, one launch (start us, length us, event | category | flops | bytes accessed | tf_op | source)
XLA Modules:
  0.0 435.5 jit_solution(13767479986867056603)
XLA Ops:
  7.2 0.0 copy-start
  7.2 0.8 fusion.13
  8.0 1.6 gather_fusion
  9.6 0.7 fusion.12
  10.2 0.1 fusion.6
  10.3 0.2 reduce_window_sum.11
  10.5 0.2 select_reduce_fusion
  10.7 0.7 fusion.11
  11.4 0.0 copy-done
  11.4 2.6 convolution_convert_fusion
  14.0 7.1 %reshape.47 = bf16[64,3,8192]{2,1,0:T(4,128)(2,1)} reshape(bf16[192,8192]{1,0:T(8,128)(2,1)} %convolution_convert_fusion) | data formatting | bytes 6291456 | tf_op jit(solution)/shard_map/reshape | solution.py:44
  21.0 0.0 copy-start.3
  21.0 20.0 %all-to-all-start.1 = ((bf16[64,3,8192]{2,1,0:T(4,128)(2,1)}), bf16[64,3,8192]{2,1,0:T(4,128)(2,1)}, u32[]{:S(2)}, u32[]{:S(2)}) async-start(bf16[64,3,8192]{2,1,0:T(4,128)(2,1)} %reshape.47), calls=%async_computation.1 | async-start | bytes 8388608 | tf_op jit(solution)/shard_map/all_to_all | solution.py:47
  41.0 0.0 copy-done.3
  41.0 0.2 convolution_convert_fusion.2
  41.2 0.8 reshape.51
  42.1 96.4 %all-to-all-done.1 = bf16[64,3,8192]{2,1,0:T(4,128)(2,1)} async-done(((bf16[64,3,8192]{2,1,0:T(4,128)(2,1)}), bf16[64,3,8192]{2,1,0:T(4,128)(2,1)}, u32[]{:S(2)}, u32[]{:S(2)}) %all-to-all-start.1) | async-done | bytes 3145760 | tf_op jit(solution)/shard_map/all_to_all | solution.py:47
  138.4 10.1 %all-to-all-start.3 = ((bf16[64,3,512]{2,1,0:T(4,128)(2,1)}), bf16[64,3,512]{2,1,0:T(4,128)(2,1)S(1)}, u32[]{:S(2)}, u32[]{:S(2)}) async-start(bf16[64,3,512]{2,1,0:T(4,128)(2,1)} %reshape.51), calls=%async_computation.3 | async-start | bytes 524288 | tf_op jit(solution)/shard_map/all_to_all | solution.py:67
  148.5 0.0 copy-start.1
  148.5 7.5 %reshape.48 = bf16[192,8192]{1,0:T(8,128)(2,1)} reshape(bf16[64,3,8192]{2,1,0:T(4,128)(2,1)} %all-to-all-done.1) | data formatting | bytes 6291456 | tf_op jit(solution)/shard_map/reshape | solution.py:48
  156.1 0.0 copy-done.1
  156.1 0.0 copy-start.2
  156.1 0.0 copy-start.4
  156.1 3.0 convolution_convert_fusion.4
  159.1 0.0 copy-done.2
  159.1 0.2 convolution_convert_fusion.1
  159.4 0.1 reshape.49
  159.5 2.7 all-to-all-done.3
  162.2 25.4 %all_to_all.20 = bf16[64,3,512]{2,1,0:T(4,128)(2,1)S(1)} all-to-all(bf16[64,3,512]{2,1,0:T(4,128)(2,1)S(1)} %reshape.49), channel_id=1, replica_groups=mesh['fsdp'=64,'dp'=8] {'fsdp'}, dimensions={0} | all-to-all | bytes 393216 | tf_op jit(solution)/shard_map/all_to_all | solution.py:57
  187.5 0.0 copy-done.4
  187.5 4.3 stack.2
  191.8 23.4 %all-to-all-start = ((bf16[512,16,512]{2,1,0:T(8,128)(2,1)}), bf16[512,16,512]{2,1,0:T(8,128)(2,1)}, u32[]{:S(2)}, u32[]{:S(2)}) async-start(bf16[512,16,512]{2,1,0:T(8,128)(2,1)} %stack.2), calls=%async_computation | async-start | bytes 16777216 | tf_op jit(solution)/shard_map/all_to_all | solution.py:25
  215.3 0.0 reduce-scatter.7.cloned.1.call-start
  215.3 0.2 reshape.52
  215.5 1.0 convolution_bitcast_fusion
  216.5 0.0 reduce-scatter.7.cloned.1.call-update
  216.5 0.0 copy-start.5
  216.5 0.0 reduce-scatter.5.cloned.1.call-start
  216.6 4.2 fusion.1
  220.7 0.0 reduce-scatter.5.cloned.1.call-update
  220.8 0.0 copy-done.5
  220.8 40.7 %reduce-scatter.7.cloned.1.call-done = f32[64,64]{1,0:T(8,128)} async-done(((f32[512,64]{1,0:T(8,128)}), f32[64,64]{1,0:T(8,128)}) %reduce-scatter.7.cloned.1.call-update) | async-done | bytes 16400
  261.4 1.5 copy.12
  262.9 0.2 reshape.50
  263.1 160.1 %all-to-all-done = bf16[512,16,512]{2,1,0:T(8,128)(2,1)} async-done(((bf16[512,16,512]{2,1,0:T(8,128)(2,1)}), bf16[512,16,512]{2,1,0:T(8,128)(2,1)}, u32[]{:S(2)}, u32[]{:S(2)}) %all-to-all-start) | async-done | bytes 8388640 | tf_op jit(solution)/shard_map/all_to_all | solution.py:25
  423.2 4.6 %convolution_add_fusion.1 = f32[128,512]{1,0:T(8,128)S(1)} fusion(bf16[128,8192]{1,0:T(8,128)(2,1)S(1)} %copy-done, bf16[8192,512]{1,0:T(8,128)(2,1)} %bitcast, f32[512]{0:T(512)S(1)} %convert_element_type.25), kind=kOutput, calls=%fused_computation.6 | convolution fusion | flops 1073807360 | bytes 10749952 | tf_op jit(solution)/shard_map/dot_general | solution.py:22
  427.8 0.9 fusion
  428.7 0.0 reduce-scatter.5.cloned.1.call-done
  (2 shorter events, 0.0 us)
Async XLA Ops:
  7.2 4.2 copy-start
  21.0 20.0 %copy-start.3 = (bf16[128,512]{1,0:T(8,128)(2,1)S(1)}, bf16[128,512]{1,0:T(8,128)(2,1)}, u32[]{:S(2)}) copy-start(bf16[128,512]{1,0:T(8,128)(2,1)} %param.15) | copy-start | bytes 393220
  21.0 117.4 %all-to-all-start.1 = ((bf16[64,3,8192]{2,1,0:T(4,128)(2,1)}), bf16[64,3,8192]{2,1,0:T(4,128)(2,1)}, u32[]{:S(2)}, u32[]{:S(2)}) async-start(bf16[64,3,8192]{2,1,0:T(4,128)(2,1)} %reshape.47), calls=%async_computation.1 | async-start | bytes 8388608 | tf_op jit(solution)/shard_map/all_to_all | solution.py:47
  138.4 23.7 %all-to-all-start.3 = ((bf16[64,3,512]{2,1,0:T(4,128)(2,1)}), bf16[64,3,512]{2,1,0:T(4,128)(2,1)S(1)}, u32[]{:S(2)}, u32[]{:S(2)}) async-start(bf16[64,3,512]{2,1,0:T(4,128)(2,1)} %reshape.51), calls=%async_computation.3 | async-start | bytes 524288 | tf_op jit(solution)/shard_map/all_to_all | solution.py:67
  148.5 7.6 %copy-start.1 = (bf16[1,8192,64]{1,2,0:T(8,128)(2,1)S(1)}, bf16[1,8192,64]{1,2,0:T(8,128)(2,1)}, u32[]{:S(2)}) copy-start(bf16[1,8192,64]{1,2,0:T(8,128)(2,1)} %param.13) | copy-start | bytes 3145732
  156.1 3.1 copy-start.2
  156.1 31.4 %copy-start.4 = (bf16[16,512]{1,0:T(8,128)(2,1)S(1)}, bf16[16,512]{1,0:T(8,128)(2,1)}, u32[]{:S(2)}) copy-start(bf16[16,512]{1,0:T(8,128)(2,1)} %param.11) | copy-start | bytes 49156
  191.8 231.3 %all-to-all-start = ((bf16[512,16,512]{2,1,0:T(8,128)(2,1)}), bf16[512,16,512]{2,1,0:T(8,128)(2,1)}, u32[]{:S(2)}, u32[]{:S(2)}) async-start(bf16[512,16,512]{2,1,0:T(8,128)(2,1)} %stack.2), calls=%async_computation | async-start | bytes 16777216 | tf_op jit(solution)/shard_map/all_to_all | solution.py:25
  215.3 46.2 %reduce-scatter.7.cloned.1.call-start = ((), (), s32[]{:S(2)}) async-start(), calls=%async_computation.7 | async-start | bytes 294912
  216.5 4.3 copy-start.5
  216.5 212.2 %reduce-scatter.5.cloned.1.call-start = ((), (), s32[]{:S(2)}) async-start(), calls=%async_computation.6 | async-start | bytes 2359296 | tf_op jit(solution)/shard_map/reduce_scatter | solution.py:82
Sparse Core Ops, SparseCore 0:
  218.9 42.5 reduce-scatter.6
  264.8 100.5 reduce-scatter.4
